TPU v7x, 32 devices: a whole 2x2x4 slice. The times are simulated.
32 devices in a mesh: seek: 4 (over z), emp: 8 (over y, x, core).
Axes of the slice: x: 2, y: 2, z: 4, core: 2. Of those that a mesh axis runs over, the one named last changes fastest.
Arguments:
- seek_region: int32 [64], replicated, may hold values from 0 to 7, as said below
- emp_region: int32 [64], replicated, may hold values from 0 to 7
- seeker_emb: bfloat16 [32768, 256], P('seek'), may hold values from -52 to 52
- employer_emb: bfloat16 [32768, 256], P('emp'), may hold values from -6 to 6
- bilinear: bfloat16 [256, 256], replicated, may hold values from -0.375 to 0.375
- logged_emp: int32 [32768], P('seek'), may hold values from 0 to 32767, as said below
- logged_seeker: int32 [32768], P('emp'), may hold values from 0 to 32767, as said below
- seek_weight: float32 [32768], P('seek'), may hold values from 0.2 to 5
- emp_weight: float32 [32768], P('emp'), may hold values from 0.2 to 5
Outputs:
- seeker_grad: float32 [32768, 256], P(('seek', 'emp'))
- employer_grad: float32 [32768, 256], P(('emp', 'seek'))
- bilinear_grad: float32 [256, 256], replicated
Inputs may be any that keep to these rules, and one draw needn't show every extreme that they name: `seek_region`: every region holds at least one seeker block and one employer block. `logged_emp`: each seeker's logged employer lies in a block of the seeker's region. `logged_seeker`: each employer's logged seeker lies in a block of the employer's region.
All inputs are finite; a program needn't handle non-finite values.
Results may differ from a plain program's by a relative error of at most 0.012.
The roundings to bfloat16 on the way count: a program that leaves them out, or rounds other values in their place, can miss the bound.
Values sent between devices are 32-bit elements; how exact they have to be, the bound alone decides.
A program may use at most 128 MiB of HBM per device.

v0:
```python
import jax
import jax.numpy as jnp
from jax import lax
from jax.sharding import PartitionSpec as P

E = 256
BLK = 512


big_value = 1e30


def tile_scores(rows, cols):
    raw = lax.dot_general(rows, cols, (((1,), (1,)), ((), ())), preferred_element_type=jnp.float32)
    return raw * E ** (-0.5)


def partial_stats(masked):
    top = jnp.max(masked, axis=1)
    total = jnp.sum(jnp.where(True, jnp.exp(masked - top[:, None]), 0.0), axis=1)
    ctop = jnp.max(masked, axis=0)
    ctotal = jnp.sum(jnp.where(True, jnp.exp(masked - ctop[None, :]), 0.0), axis=0)
    return (top, total, ctop, ctotal)


def combine(first, second):
    new_top = jnp.maximum(first[0], second[0])
    new_total = first[1] * jnp.exp(first[0] - new_top) + second[1] * jnp.exp(second[0] - new_top)
    return (new_top, new_total)


def tile_grad(
    masked, row_top, row_total, col_top, col_total, row_hit, col_hit, weight_rows, weight_cols
):
    policy = jnp.exp(masked - row_top[:, None]) / row_total[:, None]
    other = jnp.exp(masked - col_top[None, :]) / col_total[None, :]
    grad = weight_rows[:, None] * (policy - row_hit) + weight_cols[None, :] * (other - col_hit)
    return (jnp.where(True, grad, 0.0) * E ** (-0.5)).astype(jnp.bfloat16)


def body(
    seek_region,
    emp_region,
    seeker_emb,
    employer_emb,
    bilinear,
    logged_emp,
    logged_seeker,
    seek_weight,
    emp_weight,
):
    seek_pos = lax.axis_index("seek")
    emp_pos = lax.axis_index("emp")
    seekers = seeker_emb.shape[0]
    employers = employer_emb.shape[0]
    nblocks = seekers // BLK
    eblocks = employers // BLK
    own_seek = lax.dynamic_slice_in_dim(seek_region, seek_pos * nblocks, nblocks)
    own_emp = lax.dynamic_slice_in_dim(emp_region, emp_pos * eblocks, eblocks)
    listed = own_seek[:, None] == own_emp[None, :]
    proj = jnp.dot(seeker_emb, bilinear, preferred_element_type=jnp.float32).astype(jnp.bfloat16)
    proj_blocks = proj.reshape(nblocks, BLK, E)
    block_ids = jnp.arange(nblocks, dtype=jnp.int32)
    local_emp = logged_emp - emp_pos * employers
    local_seek = logged_seeker - seek_pos * seekers
    row_index = jnp.arange(BLK, dtype=jnp.int32)
    empty_rows = jnp.full((BLK,), -big_value, jnp.float32)
    zero_rows = jnp.zeros((BLK,), jnp.float32)

    def first_pass(carry, xs):
        rows, flags = xs
        col_tops, col_totals = carry
        top, total = (empty_rows, zero_rows)
        new_tops = []
        new_totals = []
        for col in range(eblocks):
            cols = employer_emb[col * BLK : (col + 1) * BLK]

            def first_active(state, rows=rows, cols=cols):
                part_top, part_total, ctop, ctotal = partial_stats(tile_scores(rows, cols))
                row_state = combine((state[0], state[1]), (part_top, part_total))
                col_state = combine((state[2], state[3]), (ctop, ctotal))
                return (row_state[0], row_state[1], col_state[0], col_state[1])

            def first_skipped(state):
                return state

            top, total, ctop, ctotal = lax.cond(
                flags[col],
                first_active,
                first_skipped,
                (top, total, col_tops[col], col_totals[col]),
            )
            new_tops.append(ctop)
            new_totals.append(ctotal)
        return ((tuple(new_tops), tuple(new_totals)), (top, total))

    init = (
        tuple((empty_rows for col in range(eblocks))),
        tuple((zero_rows for col in range(eblocks))),
    )
    (top_parts, total_parts), (row_top, row_total) = lax.scan(
        first_pass, init, (proj_blocks, listed)
    )
    col_top = jnp.concatenate(top_parts)
    col_total = jnp.concatenate(total_parts)
    row_top = row_top.reshape(seekers)
    row_total = row_total.reshape(seekers)
    row_peak = lax.pmax(row_top, "emp")
    row_total = lax.psum(row_total * jnp.exp(row_top - row_peak), "emp")
    row_top = row_peak
    col_peak = lax.pmax(col_top, "seek")
    col_total = lax.psum(col_total * jnp.exp(col_top - col_peak), "seek")
    col_top = col_peak
    xs = (
        block_ids,
        proj_blocks,
        listed,
        row_top.reshape(nblocks, BLK),
        row_total.reshape(nblocks, BLK),
        local_emp.reshape(nblocks, BLK),
        seek_weight.reshape(nblocks, BLK),
    )

    def second_pass(carry, xs):
        index, rows, flags, top, total, logged_rows, weight_rows = xs
        seek_ids = index * BLK + row_index
        pulled = jnp.zeros((BLK, E), jnp.float32)
        backs = []
        for col in range(eblocks):
            start = col * BLK
            cols = employer_emb[start : start + BLK]

            def second_active(state, rows=rows, cols=cols, start=start):
                masked = tile_scores(rows, cols)
                row_hit = (logged_rows[:, None] == (start + row_index)[None, :]).astype(jnp.float32)
                col_hit = (local_seek[start : start + BLK][None, :] == seek_ids[:, None]).astype(
                    jnp.float32
                )
                dscore = tile_grad(
                    masked,
                    top,
                    total,
                    col_top[start : start + BLK],
                    col_total[start : start + BLK],
                    row_hit,
                    col_hit,
                    weight_rows,
                    emp_weight[start : start + BLK],
                )
                pull = jnp.dot(dscore, cols, preferred_element_type=jnp.float32)
                back = lax.dot_general(
                    dscore, rows, (((0,), (0,)), ((), ())), preferred_element_type=jnp.float32
                )
                return (state[0] + pull, state[1] + back)

            def second_skipped(state):
                return state

            pulled, back = lax.cond(flags[col], second_active, second_skipped, (pulled, carry[col]))
            backs.append(back)
        return (tuple(backs), pulled)

    init = tuple((jnp.zeros((BLK, E), jnp.float32) for col in range(eblocks)))
    back_parts, pulled = lax.scan(second_pass, init, xs)
    employer_part = jnp.concatenate(back_parts, axis=0)
    pulled = pulled.reshape(seekers, E)
    pulled_share = lax.psum_scatter(pulled, "emp", scatter_dimension=0, tiled=True).astype(
        jnp.bfloat16
    )
    employer_grad = lax.psum_scatter(employer_part, "seek", scatter_dimension=0, tiled=True)
    share = pulled_share.shape[0]
    own_rows = lax.dynamic_slice_in_dim(seeker_emb, emp_pos * share, share, 0)
    seeker_grad = lax.dot_general(
        pulled_share, bilinear, (((1,), (1,)), ((), ())), preferred_element_type=jnp.float32
    )
    bilinear_part = lax.dot_general(
        own_rows, pulled_share, (((0,), (0,)), ((), ())), preferred_element_type=jnp.float32
    )
    bilinear_grad = lax.psum(bilinear_part, ("seek", "emp"))
    return (seeker_grad, employer_grad, bilinear_grad)


def solution(mesh):
    return jax.shard_map(
        body,
        mesh=mesh,
        in_specs=(
            P(),
            P(),
            P("seek", None),
            P("emp", None),
            P(),
            P("seek"),
            P("emp"),
            P("seek"),
            P("emp"),
        ),
        out_specs=(P(("seek", "emp"), None), P(("emp", "seek"), None), P()),
        check_vma=False,
    )
```

profile of v0, /device:TPU:0, one launch (start us, length us, event | category | flops | bytes accessed | tf_op | source)
XLA Modules:
  0.0 951.1 jit_solution(9743435945648392097)
XLA Ops:
  8.7 1.4 reshape.200
  11.6 5.6 convolution_convert_fusion
  17.3 121.0 %while.75 = (s32[]{:T(128)}, f32[512]{0:T(512)S(1)}, f32[512]{0:T(512)S(1)}, f32[512]{0:T(512)S(1)}, f32[512]{0:T(512)S(1)}, /*index=5*/f32[512]{0:T(512)S(1)}, ...) while((s32[]{:T(128)}, f32[512]{0:T(512)S(1)}, ...), condition=%wide.region_49.50_spmd, body=%wide.region_0.49_spmd.sunk | while | flops 1088454656 | bytes 21796036 | solution.py:102
  138.5 27.0 %pmax.15 = f32[4096]{0:T(1024)S(1)} all-reduce(f32[4096]{0:T(1024)S(1)} %constant_dynamic-update-slice_fusion.11), channel_id=1, replica_groups=mesh['seek'=4,'emp'=8] {'seek'}, use_global_device_ids=true, to_apply=%region_52.53 | all-reduce | flops 4096 | bytes 32768 | tf_op jit(solution)/shard_map/pmax | solution.py:112
  165.5 16.1 %psum.22 = f32[4096]{0:T(1024)} all-reduce(f32[4096]{0:T(1024)S(1)} %exponential_multiply_fusion.1), channel_id=1, replica_groups=mesh['seek'=4,'emp'=8] {'seek'}, use_global_device_ids=true, to_apply=%region_53.54 | all-reduce | flops 4096 | bytes 32768 | tf_op jit(solution)/shard_map/psum | solution.py:113
  181.7 26.8 %pmax.14 = f32[8192]{0:T(1024)S(1)} all-reduce(f32[8192]{0:T(1024)S(1)} %bitcast.134), channel_id=1, replica_groups=mesh['seek'=4,'emp'=8] {'emp'}, use_global_device_ids=true, to_apply=%region_50.51 | all-reduce | flops 8192 | bytes 65536 | tf_op jit(solution)/shard_map/pmax | solution.py:109
  209.1 23.9 %psum.21 = f32[16,512]{1,0:T(8,128)} all-reduce(f32[16,512]{1,0:T(8,128)S(1)} %reshape.199), channel_id=1, replica_groups=mesh['seek'=4,'emp'=8] {'emp'}, use_global_device_ids=true, to_apply=%region_51.52 | all-reduce | flops 8192 | bytes 65536 | tf_op jit(solution)/shard_map/psum | solution.py:110
  240.0 291.9 %while.76 = (s32[]{:T(128)}, f32[512,256]{1,0:T(8,128)}, f32[512,256]{1,0:T(8,128)}, f32[512,256]{1,0:T(8,128)}, f32[512,256]{1,0:T(8,128)}, /*index=5*/f32[512,...) while((s32[]{:T(128)}, f32[512,256]{1,0:T(8,128)}, ...), condition=%wide.region_71.72_spmd.clone.clone, body=%wide.region_54.71_spmd.clone.clone.sunk | while | flops 3256750080 | bytes 68503416 | solution.py:165
  242.5 1.3 constant_dynamic-slice_fusion.13
  252.6 6.8 conditional.57
  255.3 1.8 multiply_convert_fusion.1
  259.4 6.8 conditional.61
  262.1 1.8 multiply_convert_fusion.5
  283.2 1.3 constant_dynamic-slice_fusion.13
  306.9 6.8 conditional.57
  309.7 1.8 multiply_convert_fusion.1
  313.7 6.8 conditional.61
  316.4 1.8 multiply_convert_fusion.5
  323.9 1.3 constant_dynamic-slice_fusion.13
  334.0 6.8 conditional.60
  336.8 1.8 multiply_convert_fusion.4
  344.2 1.3 constant_dynamic-slice_fusion.13
  357.8 1.3 constant_dynamic-slice_fusion.13
  371.4 1.3 constant_dynamic-slice_fusion.13
  381.5 6.8 conditional.57
  384.3 1.8 multiply_convert_fusion.1
  388.3 6.8 conditional.61
  391.1 1.8 multiply_convert_fusion.5
  398.5 1.3 constant_dynamic-slice_fusion.13
  412.1 1.3 constant_dynamic-slice_fusion.13
  425.8 1.3 constant_dynamic-slice_fusion.13
  436.0 6.8 conditional.62
  438.7 1.8 multiply_convert_fusion.6
  446.1 1.3 constant_dynamic-slice_fusion.13
  459.8 1.3 constant_dynamic-slice_fusion.13
  473.4 1.3 constant_dynamic-slice_fusion.13
  497.2 6.8 conditional.62
  500.0 1.8 multiply_convert_fusion.6
  517.5 6.8 conditional.57
  520.2 1.8 multiply_convert_fusion.1
  524.3 6.8 conditional.61
  527.0 1.8 multiply_convert_fusion.5
  539.9 191.6 %reduce-scatter.3.cloned.1.call-done = f32[1024,256]{1,0:T(8,128)} async-done(((f32[8192,256]{1,0:T(8,128)}), f32[1024,256]{1,0:T(8,128)}) %reduce-scatter.3.cloned.1.call-update) | async-done | bytes 1048592 | tf_op jit(solution)/shard_map/reduce_scatter | solution.py:168
  731.5 2.5 fusion.28
  734.0 1.3 fusion.31
  735.3 75.9 %reduce-scatter.5.cloned.1.call-done = f32[1024,256]{1,0:T(8,128)} async-done(((f32[4096,256]{1,0:T(8,128)}), f32[1024,256]{1,0:T(8,128)}) %reduce-scatter.5.cloned.1.call-update) | async-done | bytes 1048592 | tf_op jit(solution)/shard_map/reduce_scatter | solution.py:171
  811.2 131.7 %all-reduce.2.cloned.1.call-done = f32[256,256]{1,0:T(8,128)} async-done(((f32[256,256]{1,0:T(8,128)}), f32[256,256]{1,0:T(8,128)}) %all-reduce.2.cloned.1.call-update) | async-done | bytes 262160 | tf_op jit(solution)/shard_map/psum | solution.py:180
  942.9 1.7 copy.230
  (771 shorter events, 231.2 us)
Async XLA Ops:
  7.2 4.4 copy-start
  7.2 724.3 %reduce-scatter.3.cloned.1.call-start = ((), (), s32[]{:S(2)}) async-start(), calls=%async_computation.2 | async-start | bytes 9437184 | tf_op jit(solution)/shard_map/reduce_scatter | solution.py:168
  11.6 5.7 copy-start.1
  17.3 215.7 %copy-start.25 = (s32[4096]{0:T(1024)S(1)}, s32[4096]{0:T(1024)}, u32[]{:S(2)}) copy-start(s32[4096]{0:T(1024)} %param.51) | copy-start | bytes 49156
  165.4 68.2 %copy-start.24 = (f32[4096]{0:T(1024)}, f32[4096]{0:T(1024)S(1)}, u32[]{:S(2)}) copy-start(f32[4096]{0:T(1024)S(1)} %pmax.15) | copy-start | bytes 49156
  257.2 1.0 copy-start.17
  258.6 0.8 copy-start.18
  264.0 1.0 copy-start.5
  265.4 0.8 copy-start.6
  311.5 1.0 copy-start.17
  312.9 0.8 copy-start.18
  318.3 1.0 copy-start.5
  319.7 0.8 copy-start.6
  338.6 1.0 copy-start.8
  340.0 0.8 copy-start.9
  386.1 1.0 copy-start.17
  387.5 0.8 copy-start.18
  392.9 1.0 copy-start.5
  394.3 0.8 copy-start.6
  440.6 1.0 copy-start.2
  442.0 0.8 copy-start.3
  501.8 1.0 copy-start.2
  503.2 0.8 copy-start.3
  522.1 1.0 copy-start.17
  523.5 0.8 copy-start.18
  528.8 1.0 copy-start.5
  530.2 0.8 copy-start.6
  531.9 1.0 copy-start.22
  531.9 1.9 copy-start.19
  531.9 2.8 copy-start.16
  531.9 3.6 copy-start.13
  532.0 279.2 %reduce-scatter.5.cloned.1.call-start = ((), (), s32[]{:S(2)}) async-start(), calls=%async_computation.3 | async-start | bytes 5242880 | tf_op jit(solution)/shard_map/reduce_scatter | solution.py:171
  532.9 3.5 copy-start.10
  533.8 3.4 copy-start.7
  534.7 3.4 copy-start.4
  539.8 403.1 %all-reduce.2.cloned.1.call-start = ((), (), s32[]{:S(2)}) async-start(), calls=%async_computation.4 | async-start | bytes 524288 | tf_op jit(solution)/shard_map/psum | solution.py:180
  731.5 2.5 copy-start.23
Sparse Core Ops, SparseCore 0:
  532.1 199.3 reduce-scatter.2
  734.4 76.7 reduce-scatter.4
  817.3 125.5 all-reduce.1
where the time goes:
time: 960 us; the launch traced here: 951 us
  waiting for transfers between devices  399 us (42%)
  local copies, waits for them, and re-layouts  208 us (22%)
  loops' own time  179 us (19%)
  blocking collectives  93.7 us (10%)
  matrix products  41.3 us (4%)
  other arithmetic  15.3 us (2%)
  between operations  14.1 us (1%)
    reduce_scatter x1, waiting for transfers between devices, body(): lax.psum_scatter(pulled, 'emp', scatter_dimension=0, tiled=True)  192 us
    psum x1, waiting for transfers between devices, body(): bilinear_grad = lax.psum(bilinear_part, ('seek', 'emp'))  132 us
    another operation x1, loops' own time, body(): back_parts, pulled = lax.scan(second_pass, init, xs)  92.9 us
    another operation x1, loops' own time, body(): lax.scan(first_pass, init, (proj_blocks, listed))  80.8 us
    reduce_scatter x1, waiting for transfers between devices, body(): lax.psum_scatter(employer_part, 'seek', scatter_dimension=0, tiled=True)  75.9 us
    dynamic_slice x64, local copies, waits for them, and re-layouts, body(): back_parts, pulled = lax.scan(second_pass, init, xs)  72.1 us
    squeeze x32, local copies, waits for them, and re-layouts, body(): lax.scan(first_pass, init, (proj_blocks, listed))  31.1 us
    pmax x1, blocking collectives, body(): col_peak = lax.pmax(col_top, 'seek')  27 us
  transfers between devices with their start and end apart: 3, of which 3 were waited for; matrix products, arithmetic and copies ran while one was open for 1% of the time, Pallas kernels for 0%

commit v1 on v0

v1 whole, which is shorter than its diff:
```python
import functools

import jax
import jax.numpy as jnp
from jax import lax
from jax.experimental import pallas as pl
from jax.experimental.pallas import tpu as pltpu
from jax.sharding import PartitionSpec as P

E = 256
BLK = 512
LANES = 128
ROWS = 64
GROUPS = BLK // LANES
LOW = -1.0e30
TO_LOG2 = 1.4426950408889634 * E ** (-0.5)
VMEM_LIMIT = 56 * 1024 * 1024


def nt_dot(a, b):
    return lax.dot_general(a, b, (((1,), (1,)), ((), ())), preferred_element_type=jnp.float32)


def tn_dot(a, b):
    return lax.dot_general(a, b, (((0,), (0,)), ((), ())), preferred_element_type=jnp.float32)


def block_ds(index, size):
    return pl.ds(pl.multiple_of(index * size, size), size)


def stats_kernel(
    nblocks, eblocks, flags, seeker, employer, bilinear,
    proj, row_stats, col_stats,
    score, row_max, row_sum, col_max, col_sum,
):
    col_max[...] = jnp.full_like(col_max, LOW)
    col_sum[...] = jnp.zeros_like(col_sum)

    def per_row(i, carry):
        rows_at = block_ds(i, BLK)
        proj[rows_at, :] = jnp.dot(
            seeker[rows_at, :], bilinear[...], preferred_element_type=jnp.float32
        ).astype(jnp.bfloat16)
        row_max[...] = jnp.full_like(row_max, LOW)
        row_sum[...] = jnp.zeros_like(row_sum)

        def per_col(j, carry):
            @pl.when(flags[i * eblocks + j] != 0)
            def _():
                cols = employer[block_ds(j, BLK), :]
                half = BLK // 2
                for h in range(2):
                    left = proj[pl.ds(pl.multiple_of(i * BLK + h * half, half), half), :]
                    score[h * half : (h + 1) * half, :] = nt_dot(left, cols)
                cm = col_max[j]
                cs = col_sum[j]
                for c in range(BLK // ROWS):
                    part = slice(c * ROWS, (c + 1) * ROWS)
                    s = score[part, :] * TO_LOG2
                    tall = s.reshape(ROWS // 8, 8, BLK)
                    cm_new = jnp.maximum(cm, jnp.max(tall, axis=0))
                    cs = cs * jnp.exp2(cm - cm_new) + jnp.sum(
                        jnp.exp2(tall - cm_new[None]), axis=0
                    )
                    cm = cm_new
                    old = row_max[part, :]
                    pieces = [s[:, g * LANES : (g + 1) * LANES] for g in range(GROUPS)]
                    new = functools.reduce(jnp.maximum, pieces, old)
                    total = row_sum[part, :] * jnp.exp2(old - new)
                    for piece in pieces:
                        total = total + jnp.exp2(piece - new)
                    row_max[part, :] = new
                    row_sum[part, :] = total
                col_max[j] = cm
                col_sum[j] = cs

            return carry

        lax.fori_loop(0, eblocks, per_col, 0)
        lane_max = row_max[...]
        top = jnp.max(lane_max, axis=1, keepdims=True)
        total = jnp.sum(row_sum[...] * jnp.exp2(lane_max - top), axis=1, keepdims=True)
        row_stats[0, pl.ds(i, 1), :] = jnp.broadcast_to(top, (BLK, LANES)).T[0:1]
        row_stats[1, pl.ds(i, 1), :] = jnp.broadcast_to(total, (BLK, LANES)).T[0:1]
        return carry

    lax.fori_loop(0, nblocks, per_row, 0)
    for j in range(eblocks):
        cm = col_max[j]
        top = jnp.max(cm, axis=0, keepdims=True)
        total = jnp.sum(col_sum[j] * jnp.exp2(cm - top), axis=0, keepdims=True)
        col_stats[0, j : j + 1, :] = top
        col_stats[1, j : j + 1, :] = total


def entry_barrier(n_seek, n_emp, me_s, me_e):
    barrier = pltpu.get_barrier_semaphore()
    for k in range(1, n_emp):
        pl.semaphore_signal(
            barrier, inc=1, device_id={"emp": lax.rem(me_e + k, n_emp)},
            device_id_type=pl.DeviceIdType.MESH,
        )
    for k in range(1, n_seek):
        pl.semaphore_signal(
            barrier, inc=1, device_id={"seek": lax.rem(me_s + k, n_seek)},
            device_id_type=pl.DeviceIdType.MESH,
        )
    pl.semaphore_wait(barrier, n_emp + n_seek - 2)


def send(src, dst, send_sem, recv_sem, axis, peer):
    return pltpu.make_async_remote_copy(
        src_ref=src, dst_ref=dst, send_sem=send_sem, recv_sem=recv_sem,
        device_id={axis: peer}, device_id_type=pl.DeviceIdType.MESH,
    )


def exchange_kernel(
    n_seek, n_emp, row_stats, col_stats, row_weight, col_weight,
    row_top, row_coef, col_top, col_coef,
    row_buf, col_buf, row_send, row_recv, col_send, col_recv,
):
    me_s = lax.axis_index("seek")
    me_e = lax.axis_index("emp")
    entry_barrier(n_seek, n_emp, me_s, me_e)
    copies = []
    for k in range(1, n_emp):
        copies.append(send(
            row_stats, row_buf.at[k], row_send.at[k], row_recv.at[k],
            "emp", lax.rem(me_e + k, n_emp),
        ))
    for k in range(1, n_seek):
        copies.append(send(
            col_stats, col_buf.at[k], col_send.at[k], col_recv.at[k],
            "seek", lax.rem(me_s + k, n_seek),
        ))
    for copy in copies:
        copy.start()
    for copy in copies:
        copy.wait()
    for own, buf, n, weight, top_out, coef_out in (
        (row_stats, row_buf, n_emp, row_weight, row_top, row_coef),
        (col_stats, col_buf, n_seek, col_weight, col_top, col_coef),
    ):
        top = own[0]
        for k in range(1, n):
            top = jnp.maximum(top, buf[k, 0])
        total = own[1] * jnp.exp2(own[0] - top)
        for k in range(1, n):
            total = total + buf[k, 1] * jnp.exp2(buf[k, 0] - top)
        top_out[...] = top
        coef_out[...] = weight[...] / total


def grad_kernel(
    nblocks, eblocks, flags, proj, employer,
    row_top, row_coef, row_weight, row_log, col_top, col_coef, col_weight, col_log,
    pulled, back,
    score, dscore, rt, rc, rw, rl,
):
    back[...] = jnp.zeros_like(back)
    row_ids = lax.broadcasted_iota(jnp.int32, (ROWS, LANES), 0).astype(jnp.float32)
    lane_ids = lax.broadcasted_iota(jnp.int32, (8, LANES), 1).astype(jnp.float32)[0:1]

    def per_row(i, carry):
        rows_at = block_ds(i, BLK)
        pulled[rows_at, :] = jnp.zeros((BLK, E), jnp.float32)
        for source, wide in ((row_top, rt), (row_coef, rc), (row_weight, rw), (row_log, rl)):
            wide[...] = jnp.broadcast_to(source[pl.ds(i, 1), :], (LANES, BLK)).T

        def per_col(j, carry):
            @pl.when(flags[i * eblocks + j] != 0)
            def _():
                cols_at = block_ds(j, BLK)
                cols = employer[cols_at, :]
                half = BLK // 2
                for h in range(2):
                    left = proj[pl.ds(pl.multiple_of(i * BLK + h * half, half), half), :]
                    score[h * half : (h + 1) * half, :] = nt_dot(left, cols)
                ct = col_top[pl.ds(j, 1), :]
                cc = col_coef[pl.ds(j, 1), :]
                cw = col_weight[pl.ds(j, 1), :]
                cl = col_log[pl.ds(j, 1), :] - (i * BLK).astype(jnp.float32)
                here = lane_ids + (j * BLK).astype(jnp.float32)
                for c in range(BLK // ROWS):
                    part = slice(c * ROWS, (c + 1) * ROWS)
                    rtc, rcc, rwc, rlc = (ref[part, :] for ref in (rt, rc, rw, rl))
                    clc = cl - float(c * ROWS)
                    for g in range(GROUPS):
                        lanes = slice(g * LANES, (g + 1) * LANES)
                        t = score[part, lanes] * TO_LOG2
                        grad = jnp.exp2(t - rtc) * rcc + jnp.exp2(t - ct[:, lanes]) * cc[:, lanes]
                        grad = jnp.where(rlc == here + float(g * LANES), grad - rwc, grad)
                        grad = jnp.where(clc[:, lanes] == row_ids, grad - cw[:, lanes], grad)
                        dscore[part, lanes] = grad.astype(jnp.bfloat16)
                d = dscore[...]
                pulled[rows_at, :] += jnp.dot(d, cols, preferred_element_type=jnp.float32)
                back[cols_at, :] += tn_dot(d, proj[rows_at, :])

            return carry

        lax.fori_loop(0, eblocks, per_col, 0)
        return carry

    lax.fori_loop(0, nblocks, per_row, 0)


def reduce_kernel(
    n_seek, n_emp, pulled, back, own_rows, bilinear,
    seeker_grad, employer_grad, bilinear_grad,
    pair_buf, emp_buf, right_buf, left_buf, bil, bil_emp, bil_seek, bil_all,
    pair_send, pair_recv, emp_send, emp_recv, right_send, right_recv, left_send, left_recv,
    b1_send, b1_recv, b2_send, b2_recv, b3_send, b3_recv,
):
    me_s = lax.axis_index("seek")
    me_e = lax.axis_index("emp")
    share = pulled.shape[0] // n_emp
    eshare = back.shape[0] // n_seek
    half = n_emp // 2
    mine = me_e // 2
    parity = lax.rem(me_e, 2)
    partner = me_e + 1 - 2 * parity
    mirror = n_seek - 1 - me_s
    entry_barrier(n_seek, n_emp, me_s, me_e)

    def right_copy(k, src):
        return send(
            src, right_buf.at[k], right_send.at[k], right_recv.at[k],
            "seek", lax.rem(me_s + 1, n_seek),
        )

    def left_copy(k, src):
        return send(
            src, left_buf.at[k], left_send.at[k], left_recv.at[k],
            "seek", lax.rem(me_s + n_seek - 1, n_seek),
        )

    def line_step(k):
        for pos, make, buf, target in (
            (me_s, right_copy, right_buf, n_seek - 1 - k + me_s),
            (mirror, left_copy, left_buf, k - mirror),
        ):
            @pl.when(pos == 0)
            def _(make=make, target=target):
                make(k, back.at[block_ds(target, eshare), :]).start()

            if k > 0:
                @pl.when(jnp.logical_and(pos > 0, pos <= k))
                def _(make=make, buf=buf, target=target):
                    make(k - 1, buf.at[k - 1]).wait_recv()
                    buf[k - 1] += back[block_ds(target, eshare), :]
                    make(k, buf.at[k - 1]).start()

    line_step(0)
    pairs = []
    order = list(range(half - 1, -1, -1))
    for k in range(half):
        target = 2 * lax.rem(mine + k, half) + 1 - parity
        pairs.append(send(
            pulled.at[block_ds(target, share), :], pair_buf.at[k],
            pair_send.at[k], pair_recv.at[k], "emp", partner,
        ))
    for k in order:
        pairs[k].start()
    seconds = {}
    for k in order:
        pairs[k].wait_recv()
        target = 2 * lax.rem(mine + k, half) + parity
        pair_buf[k] += pulled[block_ds(target, share), :]
        if k > 0:
            seconds[k] = send(
                pair_buf.at[k], emp_buf.at[k], emp_send.at[k], emp_recv.at[k], "emp", target
            )
            seconds[k].start()
    for k in range(1, n_seek - 1):
        line_step(k)
    for k in seconds:
        seconds[k].wait_recv()
        pair_buf[0] += emp_buf[k]

    share_rows = pair_buf[0].astype(jnp.bfloat16)
    bil[...] = tn_dot(own_rows[...], share_rows)
    slab = E // n_emp
    b1 = []
    for k in range(1, n_emp):
        peer = lax.rem(me_e + k, n_emp)
        b1.append(send(
            bil.at[block_ds(peer, slab), :], bil_emp.at[k], b1_send.at[k], b1_recv.at[k],
            "emp", peer,
        ))
    for copy in b1:
        copy.start()
    seeker_grad[...] = nt_dot(share_rows, bilinear[...])
    own_slab = block_ds(me_e, slab)
    for copy in b1:
        copy.wait_recv()
    part = bil[own_slab, :]
    for k in range(1, n_emp):
        part = part + bil_emp[k]
    bil_seek[me_s] = part
    b2 = []
    for k in range(1, n_seek):
        b2.append(send(
            bil_seek.at[me_s], bil_seek.at[me_s], b2_send.at[k], b2_recv.at[k],
            "seek", lax.rem(me_s + k, n_seek),
        ))
    for copy in b2:
        copy.start()
    for k in range(1, n_seek):
        slot = bil_seek.at[lax.rem(me_s + n_seek - k, n_seek)]
        send(
            slot, slot, b2_send.at[k], b2_recv.at[k], "seek", lax.rem(me_s + k, n_seek)
        ).wait_recv()
    part = bil_seek[0]
    for k in range(1, n_seek):
        part = part + bil_seek[k]
    bil_all[own_slab, :] = part
    b3 = []
    for k in range(1, n_emp):
        b3.append(send(
            bil_all.at[own_slab, :], bil_all.at[own_slab, :], b3_send.at[k], b3_recv.at[k],
            "emp", lax.rem(me_e + k, n_emp),
        ))
    for copy in b3:
        copy.start()
    for k in range(1, n_emp):
        slot = bil_all.at[block_ds(lax.rem(me_e + n_emp - k, n_emp), slab), :]
        send(
            slot, slot, b3_send.at[k], b3_recv.at[k], "emp", lax.rem(me_e + k, n_emp)
        ).wait_recv()
    bilinear_grad[...] = bil_all[...]

    employer_grad[...] = back[block_ds(me_s, eshare), :]
    last = n_seek - 2
    for pos, make, buf in ((me_s, right_copy, right_buf), (mirror, left_copy, left_buf)):
        @pl.when(pos > 0)
        def _(make=make, buf=buf):
            make(last, buf.at[last]).wait_recv()
            employer_grad[...] += buf[last]

    for copy in pairs + list(seconds.values()) + b1 + b2 + b3:
        copy.wait_send()
    for k in range(n_seek - 1):
        for pos, make, buf in ((me_s, right_copy, right_buf), (mirror, left_copy, left_buf)):
            @pl.when(pos <= k)
            def _(k=k, make=make, buf=buf):
                make(k, buf.at[k]).wait_send()


def vmem():
    return pl.BlockSpec(memory_space=pltpu.VMEM)


def smem():
    return pl.BlockSpec(memory_space=pltpu.SMEM)


def f32(*shape):
    return jax.ShapeDtypeStruct(shape, jnp.float32)


def body(
    n_seek, n_emp, seek_region, emp_region, seeker_emb, employer_emb, bilinear,
    logged_emp, logged_seeker, seek_weight, emp_weight,
):
    seek_pos = lax.axis_index("seek")
    emp_pos = lax.axis_index("emp")
    seekers = seeker_emb.shape[0]
    employers = employer_emb.shape[0]
    nblocks = seekers // BLK
    eblocks = employers // BLK
    own_seek = lax.dynamic_slice_in_dim(seek_region, seek_pos * nblocks, nblocks)
    own_emp = lax.dynamic_slice_in_dim(emp_region, emp_pos * eblocks, eblocks)
    flags = (own_seek[:, None] == own_emp[None, :]).astype(jnp.int32).reshape(-1)
    row_log = (logged_emp - emp_pos * employers).astype(jnp.float32).reshape(nblocks, BLK)
    col_log = (logged_seeker - seek_pos * seekers).astype(jnp.float32).reshape(eblocks, BLK)
    scale = E ** (-0.5)
    row_weight = (seek_weight * scale).reshape(nblocks, BLK)
    col_weight = (emp_weight * scale).reshape(eblocks, BLK)

    proj, row_stats, col_stats = pl.pallas_call(
        functools.partial(stats_kernel, nblocks, eblocks),
        out_shape=(
            jax.ShapeDtypeStruct((seekers, E), jnp.bfloat16),
            f32(2, nblocks, BLK),
            f32(2, eblocks, BLK),
        ),
        in_specs=[smem()] + [vmem()] * 3,
        out_specs=(vmem(),) * 3,
        scratch_shapes=[
            pltpu.VMEM((BLK, BLK), jnp.float32),
            pltpu.VMEM((BLK, LANES), jnp.float32),
            pltpu.VMEM((BLK, LANES), jnp.float32),
            pltpu.VMEM((eblocks, 8, BLK), jnp.float32),
            pltpu.VMEM((eblocks, 8, BLK), jnp.float32),
        ],
        compiler_params=pltpu.CompilerParams(vmem_limit_bytes=VMEM_LIMIT),
        name="stats",
    )(flags, seeker_emb, employer_emb, bilinear)

    row_top, row_coef, col_top, col_coef = pl.pallas_call(
        functools.partial(exchange_kernel, n_seek, n_emp),
        out_shape=(f32(nblocks, BLK), f32(nblocks, BLK), f32(eblocks, BLK), f32(eblocks, BLK)),
        in_specs=[vmem()] * 4,
        out_specs=(vmem(),) * 4,
        scratch_shapes=[
            pltpu.VMEM((n_emp, 2, nblocks, BLK), jnp.float32),
            pltpu.VMEM((n_seek, 2, eblocks, BLK), jnp.float32),
            pltpu.SemaphoreType.DMA((n_emp,)),
            pltpu.SemaphoreType.DMA((n_emp,)),
            pltpu.SemaphoreType.DMA((n_seek,)),
            pltpu.SemaphoreType.DMA((n_seek,)),
        ],
        compiler_params=pltpu.CompilerParams(collective_id=0, has_side_effects=True),
        name="exchange",
    )(row_stats, col_stats, row_weight, col_weight)

    pulled, back = pl.pallas_call(
        functools.partial(grad_kernel, nblocks, eblocks),
        out_shape=(f32(seekers, E), f32(employers, E)),
        in_specs=[smem()] + [vmem()] * 10,
        out_specs=(vmem(),) * 2,
        scratch_shapes=[
            pltpu.VMEM((BLK, BLK), jnp.float32),
            pltpu.VMEM((BLK, BLK), jnp.bfloat16),
        ]
        + [pltpu.VMEM((BLK, LANES), jnp.float32)] * 4,
        compiler_params=pltpu.CompilerParams(vmem_limit_bytes=VMEM_LIMIT),
        name="grads",
    )(
        flags, proj, employer_emb,
        row_top, row_coef, row_weight, row_log, col_top, col_coef, col_weight, col_log,
    )

    share = seekers // n_emp
    eshare = employers // n_seek
    own_rows = lax.dynamic_slice_in_dim(seeker_emb, emp_pos * share, share, 0)
    slab = E // n_emp
    dma = pltpu.SemaphoreType.DMA
    return pl.pallas_call(
        functools.partial(reduce_kernel, n_seek, n_emp),
        out_shape=(f32(share, E), f32(eshare, E), f32(E, E)),
        in_specs=[vmem()] * 4,
        out_specs=(vmem(),) * 3,
        scratch_shapes=[
            pltpu.VMEM((n_emp // 2, share, E), jnp.float32),
            pltpu.VMEM((n_emp // 2, share, E), jnp.float32),
            pltpu.VMEM((n_seek - 1, eshare, E), jnp.float32),
            pltpu.VMEM((n_seek - 1, eshare, E), jnp.float32),
            pltpu.VMEM((E, E), jnp.float32),
            pltpu.VMEM((n_emp, slab, E), jnp.float32),
            pltpu.VMEM((n_seek, slab, E), jnp.float32),
            pltpu.VMEM((E, E), jnp.float32),
            dma((n_emp // 2,)), dma((n_emp // 2,)),
            dma((n_emp // 2,)), dma((n_emp // 2,)),
            dma((n_seek - 1,)), dma((n_seek - 1,)),
            dma((n_seek - 1,)), dma((n_seek - 1,)),
            dma((n_emp,)), dma((n_emp,)),
            dma((n_seek,)), dma((n_seek,)),
            dma((n_emp,)), dma((n_emp,)),
        ],
        compiler_params=pltpu.CompilerParams(
            collective_id=1, has_side_effects=True, vmem_limit_bytes=VMEM_LIMIT
        ),
        name="reduce",
    )(pulled, back, own_rows, bilinear)


def solution(mesh):
    return jax.shard_map(
        functools.partial(body, mesh.shape["seek"], mesh.shape["emp"]),
        mesh=mesh,
        in_specs=(
            P(),
            P(),
            P("seek", None),
            P("emp", None),
            P(),
            P("seek"),
            P("emp"),
            P("seek"),
            P("emp"),
        ),
        out_specs=(P(("seek", "emp"), None), P(("emp", "seek"), None), P()),
        check_vma=False,
    )
```

time: 960 us -> 185 us (0.19)
  waiting for transfers between devices: 399 us -> 0 us
  local copies, waits for them, and re-layouts: 208 us -> 11.7 us
  loops' own time: 179 us -> 0 us
  Pallas kernels: 0 us -> 172 us
  blocking collectives: 93.7 us -> 0 us
  matrix products: 41.3 us -> 0 us
  other arithmetic: 15.3 us -> 0.09 us
  between operations: 14.1 us -> 0.73 us
    reduce_scatter x2 -> x0, waiting for transfers between devices: 267 us -> none  [the longest x1 192 us: body(): lax.psum_scatter(pulled, 'emp', scatter_dimension=0, tiled=True)]
    another operation x258 -> x0, loops' own time: 179 us -> none  [the longest x1 92.9 us: body(): back_parts, pulled = lax.scan(second_pass, init, xs)]
    pallas_call x0 -> x4, Pallas kernels: none -> 172 us  [the longest x1 95.1 us: body(): pl.pallas_call(functools.partial(reduce_kernel, n_seek, n_emp), out_shape...]
    psum x1 -> x0, waiting for transfers between devices: 132 us -> none  [body(): bilinear_grad = lax.psum(bilinear_part, ('seek', 'emp'))]
    dynamic_slice x96 -> x1, local copies, waits for them, and re-layouts: 74.6 us -> 1.87 us  [body(): own_rows = lax.dynamic_slice_in_dim(seeker_emb, emp_pos * share, share, 0)]
    pmax x2 -> x0, blocking collectives: 53.7 us -> none  [the longest x1 27 us: body(): col_peak = lax.pmax(col_top, 'seek')]
    slice x76 -> x0, local copies, waits for them, and re-layouts: 49.6 us -> none  [the longest x16 9.95 us: second_pass(): flags[col]]
    dot_general x47 -> x0, matrix products: 41.3 us -> none  [the longest x22 24.7 us: tile_scores(): lax.dot_general(rows, cols, (((1,), (1,)), ((), ())), preferred_element_t...]
  transfers between devices with their start and end apart: 3 -> 0, of which waited for: 3 -> 0; matrix products, arithmetic and copies ran while one was open for 1% -> 0% of each run, Pallas kernels for 0% -> 0%
where the time goes in v1:
time: 185 us; the launch traced here: 184 us
  Pallas kernels  172 us (93%)
  local copies, waits for them, and re-layouts  11.7 us (6%)
    pallas_call x1, Pallas kernels, body(): pl.pallas_call(functools.partial(reduce_kernel, n_seek, n_emp), out_shape...  95.1 us
    pallas_call x1, Pallas kernels, body(): pl.pallas_call(functools.partial(grad_kernel, nblocks, eblocks), out_shap...  34.3 us
    pallas_call x1, Pallas kernels, body(): pl.pallas_call(functools.partial(stats_kernel, nblocks, eblocks), out_sha...  27.6 us
    pallas_call x1, Pallas kernels, body(): pl.pallas_call(functools.partial(exchange_kernel, n_seek, n_emp), out_sha...  14.6 us
    unnamed x13, local copies, waits for them, and re-layouts  5.29 us

profile of v1, /device:TPU:0, one launch (start us, length us, event | category | flops | bytes accessed | tf_op | source)
XLA Modules:
  0.0 184.2 jit_solution(17555486364228756273)
XLA Ops:
  0.6 0.0 copy-start.1
  0.6 0.0 copy-start.3
  0.7 0.0 copy-start.2
  0.7 0.0 copy-start.4
  0.7 0.7 dynamic_slice.10
  1.4 0.7 dynamic_slice.9
  2.2 0.1 compare_convert_fusion
  2.2 0.6 reshape.30.flags
  2.9 27.6 %stats.1 = (bf16[8192,256]{1,0:T(8,128)(2,1)}, f32[2,16,512]{2,1,0:T(8,128)}, f32[2,8,512]{2,1,0:T(8,128)}) custom-call(s32[128]{0:T(128)} %reshape.30.flags, bf16[8192,256]{1,0:T(8,128)(2,1)} %seeker.1, bf16[4096,256]{1,0:T(8,128)(2,1)} %employer.3, bf16[256,256]{1,0:T(8,128)(2,1)} %bilinear.3), custom_call_target="tpu_custom_call" | custom-call | tf_op jit(solution)/shard_map/stats/pallas_call | solution.py:382
  30.5 0.0 copy-done.1
  30.5 0.6 reshape.26.row_weight
  31.1 0.0 copy-done.3
  31.1 0.6 reshape.27.col_weight
  31.7 14.6 %exchange.1 = (f32[16,512]{1,0:T(8,128)}, f32[16,512]{1,0:T(8,128)}, f32[8,512]{1,0:T(8,128)}, f32[8,512]{1,0:T(8,128)}) custom-call(f32[2,16,512]{2,1,0:T(8,128)} %get-tuple-element.13.row_stats, f32[2,8,512]{2,1,0:T(8,128)} %get-tuple-element.14.col_stats, f32[16,512]{1,0:T(8,128)} %reshape.26.row_weight, f32[8,512]{1,0:T(8,128)} %reshape.27.col_weight), custom_call_target="tpu_custom_call" | custom-call | tf_op jit(solution)/shard_map/exchange/pallas_call | solution.py:402
  46.3 0.0 copy-done.2
  46.4 0.6 reshape.28.row_log
  47.0 0.0 copy-done.4
  47.0 0.6 reshape.29.col_log
  47.6 34.3 %grads.1 = (f32[8192,256]{1,0:T(8,128)}, f32[4096,256]{1,0:T(8,128)}) custom-call(s32[128]{0:T(128)} %reshape.30.flags, bf16[8192,256]{1,0:T(8,128)(2,1)} %get-tuple-element.12.proj, bf16[4096,256]{1,0:T(8,128)(2,1)} %employer.3, f32[16,512]{1,0:T(8,128)} %get-tuple-element.15.row_top, f32[16,512]{1,0:T(8,128)} %get-tuple-element.16.row_coef, ...), custom_call_target="tpu_custom_call" | custom-call | tf_op jit(solution)/shard_map/grads/pallas_call | solution.py:419
  81.9 1.9 %constant_dynamic-slice_fusion.own_rows = bf16[1024,256]{1,0:T(8,128)(2,1)} fusion(bf16[8192,256]{1,0:T(8,128)(2,1)} %seeker.1, s32[]{:T(128)S(6)} %select_n.11), kind=kLoop, calls=%fused_computation.5 | loop fusion | bytes 1048580 | tf_op jit(solution)/shard_map/dynamic_slice | solution.py:438
  83.8 95.1 %reduce.1 = (f32[1024,256]{1,0:T(8,128)}, f32[1024,256]{1,0:T(8,128)}, f32[256,256]{1,0:T(8,128)}) custom-call(f32[8192,256]{1,0:T(8,128)} %get-tuple-element.19.pulled, f32[4096,256]{1,0:T(8,128)} %get-tuple-element.20.back, bf16[1024,256]{1,0:T(8,128)(2,1)} %constant_dynamic-slice_fusion.own_rows, bf16[256,256]{1,0:T(8,128)(2,1)} %bilinear.3), custom_call_target="tpu_custom_call" | custom-call | tf_op jit(solution)/shard_map/reduce/pallas_call | solution.py:441
  178.9 0.0 copy-start
  178.9 2.3 %copy.15 = f32[1024,256]{1,0:T(8,128)} copy(f32[1024,256]{1,0:T(8,128)} %get-tuple-element.24) | data formatting | bytes 2097152
  181.2 2.3 %copy.16 = f32[1024,256]{1,0:T(8,128)} copy(f32[1024,256]{1,0:T(8,128)} %get-tuple-element.25) | data formatting | bytes 2097152
  183.5 0.0 copy-done
  183.5 0.7 copy.17
  (4 shorter events, 0.0 us)
Async XLA Ops:
  0.6 29.8 %copy-start.1 = (f32[8192]{0:T(1024)S(1)}, f32[8192]{0:T(1024)}, u32[]{:S(2)}) copy-start(f32[8192]{0:T(1024)} %param.16) | copy-start | bytes 98308
  0.6 30.5 %copy-start.3 = (f32[4096]{0:T(1024)S(1)}, f32[4096]{0:T(1024)}, u32[]{:S(2)}) copy-start(f32[4096]{0:T(1024)} %param.17) | copy-start | bytes 49156
  0.7 45.7 %copy-start.2 = (s32[8192]{0:T(1024)S(1)}, s32[8192]{0:T(1024)}, u32[]{:S(2)}) copy-start(s32[8192]{0:T(1024)} %param.14) | copy-start | bytes 98308
  0.7 46.3 %copy-start.4 = (s32[4096]{0:T(1024)S(1)}, s32[4096]{0:T(1024)}, u32[]{:S(2)}) copy-start(s32[4096]{0:T(1024)} %param.15) | copy-start | bytes 49156
  178.9 4.6 %copy-start = (f32[256,256]{1,0:T(8,128)S(1)}, f32[256,256]{1,0:T(8,128)}, u32[]{:S(2)}) copy-start(f32[256,256]{1,0:T(8,128)} %get-tuple-element.26) | copy-start | bytes 786436

commit v2 on v1

--- a/solution.py
+++ b/solution.py
@@ -29,63 +29,105 @@
     return pl.ds(pl.multiple_of(index * size, size), size)
 
 
+def list_pairs(seek_region, emp_region, seek_at, emp_at, nblocks, eblocks, list_i, list_j):
+    list_i[0] = nblocks
+    list_j[0] = eblocks
+
+    def visit(p, count):
+        i = p // eblocks
+        j = lax.rem(p, eblocks)
+        list_i[count + 1] = i
+        list_j[count + 1] = j
+        same = seek_region[seek_at + i] == emp_region[emp_at + j]
+        return count + same.astype(jnp.int32)
+
+    count = lax.fori_loop(0, nblocks * eblocks, visit, jnp.int32(0))
+    for k in range(1, 4):
+        list_i[count + k] = nblocks
+        list_j[count + k] = eblocks
+    list_i[nblocks * eblocks + 4] = count
+
+
 def stats_kernel(
-    nblocks, eblocks, flags, seeker, employer, bilinear,
-    proj, row_stats, col_stats,
-    score, row_max, row_sum, col_max, col_sum,
+    nblocks, eblocks, seek_region, emp_region, seeker, employer, bilinear,
+    proj, row_stats, col_stats, list_i, list_j,
+    score_a, score_b, row_max, row_sum, col_max, col_sum,
 ):
+    list_pairs(
+        seek_region, emp_region, lax.axis_index("seek") * nblocks,
+        lax.axis_index("emp") * eblocks, nblocks, eblocks, list_i, list_j,
+    )
+    count = list_i[nblocks * eblocks + 4]
     col_max[...] = jnp.full_like(col_max, LOW)
     col_sum[...] = jnp.zeros_like(col_sum)
 
-    def per_row(i, carry):
+    def project(i, carry):
         rows_at = block_ds(i, BLK)
         proj[rows_at, :] = jnp.dot(
             seeker[rows_at, :], bilinear[...], preferred_element_type=jnp.float32
         ).astype(jnp.bfloat16)
-        row_max[...] = jnp.full_like(row_max, LOW)
-        row_sum[...] = jnp.zeros_like(row_sum)
-
-        def per_col(j, carry):
-            @pl.when(flags[i * eblocks + j] != 0)
-            def _():
-                cols = employer[block_ds(j, BLK), :]
-                half = BLK // 2
-                for h in range(2):
-                    left = proj[pl.ds(pl.multiple_of(i * BLK + h * half, half), half), :]
-                    score[h * half : (h + 1) * half, :] = nt_dot(left, cols)
-                cm = col_max[j]
-                cs = col_sum[j]
-                for c in range(BLK // ROWS):
-                    part = slice(c * ROWS, (c + 1) * ROWS)
-                    s = score[part, :] * TO_LOG2
-                    tall = s.reshape(ROWS // 8, 8, BLK)
-                    cm_new = jnp.maximum(cm, jnp.max(tall, axis=0))
-                    cs = cs * jnp.exp2(cm - cm_new) + jnp.sum(
-                        jnp.exp2(tall - cm_new[None]), axis=0
-                    )
-                    cm = cm_new
-                    old = row_max[part, :]
-                    pieces = [s[:, g * LANES : (g + 1) * LANES] for g in range(GROUPS)]
-                    new = functools.reduce(jnp.maximum, pieces, old)
-                    total = row_sum[part, :] * jnp.exp2(old - new)
-                    for piece in pieces:
-                        total = total + jnp.exp2(piece - new)
-                    row_max[part, :] = new
-                    row_sum[part, :] = total
-                col_max[j] = cm
-                col_sum[j] = cs
-
-            return carry
-
-        lax.fori_loop(0, eblocks, per_col, 0)
-        lane_max = row_max[...]
+        row_max[rows_at, :] = jnp.full((BLK, LANES), LOW, jnp.float32)
+        row_sum[rows_at, :] = jnp.zeros((BLK, LANES), jnp.float32)
+        return carry
+
+    lax.fori_loop(0, nblocks, project, 0)
+    half = BLK // 2
+
+    def score_half(n, h, out):
+        i = jnp.minimum(list_i[n + 1], nblocks - 1)
+        j = jnp.minimum(list_j[n + 1], eblocks - 1)
+        left = proj[pl.ds(pl.multiple_of(i * BLK + h * half, half), half), :]
+        out[h * half : (h + 1) * half, :] = nt_dot(left, employer[block_ds(j, BLK), :])
+
+    def step(n, score, later):
+        i = list_i[n + 1]
+        j = list_j[n + 1]
+        cm = col_max[j]
+        cs = col_sum[j]
+        for c in range(BLK // ROWS):
+            if c in (0, 4):
+                score_half(n + 1, c // 4, later)
+            part = slice(c * ROWS, (c + 1) * ROWS)
+            rows_at = pl.ds(pl.multiple_of(i * BLK + c * ROWS, ROWS), ROWS)
+            s = score[part, :] * TO_LOG2
+            tall = s.reshape(ROWS // 8, 8, BLK)
+            cm_new = jnp.maximum(cm, jnp.max(tall, axis=0))
+            cs = cs * jnp.exp2(cm - cm_new) + jnp.sum(jnp.exp2(tall - cm_new[None]), axis=0)
+            cm = cm_new
+            old = row_max[rows_at, :]
+            pieces = [s[:, g * LANES : (g + 1) * LANES] for g in range(GROUPS)]
+            new = functools.reduce(jnp.maximum, pieces, old)
+            total = row_sum[rows_at, :] * jnp.exp2(old - new)
+            for piece in pieces:
+                total = total + jnp.exp2(piece - new)
+            row_max[rows_at, :] = new
+            row_sum[rows_at, :] = total
+        col_max[j] = cm
+        col_sum[j] = cs
+
+    score_half(0, 0, score_a)
+    score_half(0, 1, score_a)
+
+    def two(m, carry):
+        step(2 * m, score_a, score_b)
+        step(2 * m + 1, score_b, score_a)
+        return carry
+
+    lax.fori_loop(0, (count + 1) // 2, two, 0)
+
+    lane = lax.broadcasted_iota(jnp.int32, (BLK, LANES), 1)
+
+    def finish(i, carry):
+        rows_at = block_ds(i, BLK)
+        lane_max = row_max[rows_at, :]
         top = jnp.max(lane_max, axis=1, keepdims=True)
-        total = jnp.sum(row_sum[...] * jnp.exp2(lane_max - top), axis=1, keepdims=True)
-        row_stats[0, pl.ds(i, 1), :] = jnp.broadcast_to(top, (BLK, LANES)).T[0:1]
-        row_stats[1, pl.ds(i, 1), :] = jnp.broadcast_to(total, (BLK, LANES)).T[0:1]
+        total = jnp.sum(row_sum[rows_at, :] * jnp.exp2(lane_max - top), axis=1, keepdims=True)
+        both = jnp.where(lane == 0, top, total).T
+        row_stats[0, pl.ds(i, 1), :] = both[0:1]
+        row_stats[1, pl.ds(i, 1), :] = both[1:2]
         return carry
 
-    lax.fori_loop(0, nblocks, per_row, 0)
+    lax.fori_loop(0, nblocks, finish, 0)
     for j in range(eblocks):
         cm = col_max[j]
         top = jnp.max(cm, axis=0, keepdims=True)
@@ -117,8 +159,8 @@
 
 
 def exchange_kernel(
-    n_seek, n_emp, row_stats, col_stats, row_weight, col_weight,
-    row_top, row_coef, col_top, col_coef,
+    n_seek, n_emp, row_stats, col_stats, row_weight, col_weight, row_log, col_log,
+    row_pack, col_pack,
     row_buf, col_buf, row_send, row_recv, col_send, col_recv,
 ):
     me_s = lax.axis_index("seek")
@@ -137,11 +179,16 @@
         ))
     for copy in copies:
         copy.start()
+    for weight, log, pack in ((row_weight, row_log, row_pack), (col_weight, col_log, col_pack)):
+        for i in range(pack.shape[0]):
+            lanes = slice(i * BLK, (i + 1) * BLK)
+            pack[i, 2:3, :] = weight[:, lanes] * E ** (-0.5)
+            pack[i, 3:4, :] = log[:, lanes].astype(jnp.float32)
+            pack[i, 4:8, :] = jnp.zeros((4, BLK), jnp.float32)
     for copy in copies:
         copy.wait()
-    for own, buf, n, weight, top_out, coef_out in (
-        (row_stats, row_buf, n_emp, row_weight, row_top, row_coef),
-        (col_stats, col_buf, n_seek, col_weight, col_top, col_coef),
+    for own, buf, n, pack in (
+        (row_stats, row_buf, n_emp, row_pack), (col_stats, col_buf, n_seek, col_pack)
     ):
         top = own[0]
         for k in range(1, n):
@@ -149,74 +196,110 @@
         total = own[1] * jnp.exp2(own[0] - top)
         for k in range(1, n):
             total = total + buf[k, 1] * jnp.exp2(buf[k, 0] - top)
-        top_out[...] = top
-        coef_out[...] = weight[...] / total
+        for i in range(pack.shape[0]):
+            pack[i, 0:1, :] = top[i : i + 1]
+            pack[i, 1:2, :] = pack[i, 2:3, :] / total[i : i + 1]
 
 
 def grad_kernel(
-    nblocks, eblocks, flags, proj, employer,
-    row_top, row_coef, row_weight, row_log, col_top, col_coef, col_weight, col_log,
+    nblocks, eblocks, list_i, list_j, proj, employer, row_pack, col_pack,
     pulled, back,
-    score, dscore, rt, rc, rw, rl,
+    score_a, score_b, dscore_a, dscore_b, rt, rc, rw, rl,
 ):
-    back[...] = jnp.zeros_like(back)
+    count = list_i[nblocks * eblocks + 4]
+    row_base = (lax.axis_index("seek") * nblocks * BLK).astype(jnp.float32)
+    col_base = (lax.axis_index("emp") * eblocks * BLK).astype(jnp.float32)
+    dscore_b[...] = jnp.zeros_like(dscore_b)
     row_ids = lax.broadcasted_iota(jnp.int32, (ROWS, LANES), 0).astype(jnp.float32)
     lane_ids = lax.broadcasted_iota(jnp.int32, (8, LANES), 1).astype(jnp.float32)[0:1]
 
-    def per_row(i, carry):
+    def widen(i, carry):
         rows_at = block_ds(i, BLK)
+        tall = row_pack[i].T
+        for k, wide in enumerate((rt, rc, rw, rl)):
+            wide[rows_at, :] = jnp.broadcast_to(tall[:, k : k + 1], (BLK, LANES))
         pulled[rows_at, :] = jnp.zeros((BLK, E), jnp.float32)
-        for source, wide in ((row_top, rt), (row_coef, rc), (row_weight, rw), (row_log, rl)):
-            wide[...] = jnp.broadcast_to(source[pl.ds(i, 1), :], (LANES, BLK)).T
-
-        def per_col(j, carry):
-            @pl.when(flags[i * eblocks + j] != 0)
-            def _():
-                cols_at = block_ds(j, BLK)
-                cols = employer[cols_at, :]
-                half = BLK // 2
-                for h in range(2):
-                    left = proj[pl.ds(pl.multiple_of(i * BLK + h * half, half), half), :]
-                    score[h * half : (h + 1) * half, :] = nt_dot(left, cols)
-                ct = col_top[pl.ds(j, 1), :]
-                cc = col_coef[pl.ds(j, 1), :]
-                cw = col_weight[pl.ds(j, 1), :]
-                cl = col_log[pl.ds(j, 1), :] - (i * BLK).astype(jnp.float32)
-                here = lane_ids + (j * BLK).astype(jnp.float32)
-                for c in range(BLK // ROWS):
-                    part = slice(c * ROWS, (c + 1) * ROWS)
-                    rtc, rcc, rwc, rlc = (ref[part, :] for ref in (rt, rc, rw, rl))
-                    clc = cl - float(c * ROWS)
-                    for g in range(GROUPS):
-                        lanes = slice(g * LANES, (g + 1) * LANES)
-                        t = score[part, lanes] * TO_LOG2
-                        grad = jnp.exp2(t - rtc) * rcc + jnp.exp2(t - ct[:, lanes]) * cc[:, lanes]
-                        grad = jnp.where(rlc == here + float(g * LANES), grad - rwc, grad)
-                        grad = jnp.where(clc[:, lanes] == row_ids, grad - cw[:, lanes], grad)
-                        dscore[part, lanes] = grad.astype(jnp.bfloat16)
-                d = dscore[...]
-                pulled[rows_at, :] += jnp.dot(d, cols, preferred_element_type=jnp.float32)
-                back[cols_at, :] += tn_dot(d, proj[rows_at, :])
-
-            return carry
-
-        lax.fori_loop(0, eblocks, per_col, 0)
         return carry
 
-    lax.fori_loop(0, nblocks, per_row, 0)
+    lax.fori_loop(0, nblocks, widen, 0)
+    pulled[nblocks * BLK :, :] = jnp.zeros((BLK, E), jnp.float32)
+    back[...] = jnp.zeros_like(back)
+    half = BLK // 2
+
+    def read_at(n):
+        return (
+            jnp.minimum(list_i[n + 1], nblocks - 1), jnp.minimum(list_j[n + 1], eblocks - 1)
+        )
+
+    def score_half(n, h, out):
+        i, j = read_at(n)
+        left = proj[pl.ds(pl.multiple_of(i * BLK + h * half, half), half), :]
+        out[h * half : (h + 1) * half, :] = nt_dot(left, employer[block_ds(j, BLK), :])
+
+    def pull_half(i, jr, h, d):
+        at = pl.ds(pl.multiple_of(i * BLK + h * half, half), half)
+        pulled[at, :] += jnp.dot(
+            d[h * half : (h + 1) * half, :], employer[block_ds(jr, BLK), :],
+            preferred_element_type=jnp.float32,
+        )
+
+    def back_half(ir, j, h, d):
+        at = pl.ds(pl.multiple_of(j * BLK + h * half, half), half)
+        back[at, :] += tn_dot(d[:, h * half : (h + 1) * half], proj[block_ds(ir, BLK), :])
+
+    def step(n, score, later, d, done):
+        i, j = read_at(n)
+        old_i, old_j = list_i[n], list_j[n]
+        old_ir, old_jr = read_at(n - 1)
+        work = {
+            0: lambda: score_half(n + 1, 0, later),
+            1: lambda: pull_half(old_i, old_jr, 0, done),
+            2: lambda: pull_half(old_i, old_jr, 1, done),
+            4: lambda: score_half(n + 1, 1, later),
+            5: lambda: back_half(old_ir, old_j, 0, done),
+            6: lambda: back_half(old_ir, old_j, 1, done),
+        }
+        cols = col_pack[j]
+        ct, cc, cw = cols[0:1], cols[1:2], cols[2:3]
+        cl = cols[3:4] - (row_base + (i * BLK).astype(jnp.float32))
+        here = lane_ids + (col_base + (j * BLK).astype(jnp.float32))
+        for c in range(BLK // ROWS):
+            if c in work:
+                work[c]()
+            part = slice(c * ROWS, (c + 1) * ROWS)
+            rows_at = pl.ds(pl.multiple_of(i * BLK + c * ROWS, ROWS), ROWS)
+            rtc, rcc, rwc, rlc = (ref[rows_at, :] for ref in (rt, rc, rw, rl))
+            clc = cl - float(c * ROWS)
+            for g in range(GROUPS):
+                lanes = slice(g * LANES, (g + 1) * LANES)
+                t = score[part, lanes] * TO_LOG2
+                grad = jnp.exp2(t - rtc) * rcc + jnp.exp2(t - ct[:, lanes]) * cc[:, lanes]
+                grad = jnp.where(rlc == here + float(g * LANES), grad - rwc, grad)
+                grad = jnp.where(clc[:, lanes] == row_ids, grad - cw[:, lanes], grad)
+                d[part, lanes] = grad.astype(jnp.bfloat16)
+
+    score_half(0, 0, score_a)
+    score_half(0, 1, score_a)
+
+    def two(m, carry):
+        step(2 * m, score_a, score_b, dscore_a, dscore_b)
+        step(2 * m + 1, score_b, score_a, dscore_b, dscore_a)
+        return carry
+
+    lax.fori_loop(0, (count + 2) // 2, two, 0)
 
 
 def reduce_kernel(
-    n_seek, n_emp, pulled, back, own_rows, bilinear,
+    n_seek, n_emp, pulled, back, seeker, bilinear,
     seeker_grad, employer_grad, bilinear_grad,
     pair_buf, emp_buf, right_buf, left_buf, bil, bil_emp, bil_seek, bil_all,
     pair_send, pair_recv, emp_send, emp_recv, right_send, right_recv, left_send, left_recv,
-    b1_send, b1_recv, b2_send, b2_recv, b3_send, b3_recv,
+    b1_send, b1_recv, b2_send, b2_recv, b3_send, b3_recv, own_rows, own_sem,
 ):
     me_s = lax.axis_index("seek")
     me_e = lax.axis_index("emp")
-    share = pulled.shape[0] // n_emp
-    eshare = back.shape[0] // n_seek
+    share = seeker_grad.shape[0]
+    eshare = employer_grad.shape[0]
     half = n_emp // 2
     mine = me_e // 2
     parity = lax.rem(me_e, 2)
@@ -253,6 +336,8 @@
                     make(k, buf.at[k - 1]).start()
 
     line_step(0)
+    fetch = pltpu.make_async_copy(seeker.at[block_ds(me_e, share), :], own_rows, own_sem)
+    fetch.start()
     pairs = []
     order = list(range(half - 1, -1, -1))
     for k in range(half):
@@ -280,6 +365,7 @@
         pair_buf[0] += emp_buf[k]
 
     share_rows = pair_buf[0].astype(jnp.bfloat16)
+    fetch.wait()
     bil[...] = tn_dot(own_rows[...], share_rows)
     slab = E // n_emp
     b1 = []
@@ -364,46 +450,40 @@
     n_seek, n_emp, seek_region, emp_region, seeker_emb, employer_emb, bilinear,
     logged_emp, logged_seeker, seek_weight, emp_weight,
 ):
-    seek_pos = lax.axis_index("seek")
-    emp_pos = lax.axis_index("emp")
     seekers = seeker_emb.shape[0]
     employers = employer_emb.shape[0]
     nblocks = seekers // BLK
     eblocks = employers // BLK
-    own_seek = lax.dynamic_slice_in_dim(seek_region, seek_pos * nblocks, nblocks)
-    own_emp = lax.dynamic_slice_in_dim(emp_region, emp_pos * eblocks, eblocks)
-    flags = (own_seek[:, None] == own_emp[None, :]).astype(jnp.int32).reshape(-1)
-    row_log = (logged_emp - emp_pos * employers).astype(jnp.float32).reshape(nblocks, BLK)
-    col_log = (logged_seeker - seek_pos * seekers).astype(jnp.float32).reshape(eblocks, BLK)
-    scale = E ** (-0.5)
-    row_weight = (seek_weight * scale).reshape(nblocks, BLK)
-    col_weight = (emp_weight * scale).reshape(eblocks, BLK)
-
-    proj, row_stats, col_stats = pl.pallas_call(
+    pairs = jax.ShapeDtypeStruct((nblocks * eblocks + 5,), jnp.int32)
+
+    proj, row_stats, col_stats, list_i, list_j = pl.pallas_call(
         functools.partial(stats_kernel, nblocks, eblocks),
         out_shape=(
             jax.ShapeDtypeStruct((seekers, E), jnp.bfloat16),
             f32(2, nblocks, BLK),
             f32(2, eblocks, BLK),
+            pairs,
+            pairs,
         ),
-        in_specs=[smem()] + [vmem()] * 3,
-        out_specs=(vmem(),) * 3,
+        in_specs=[smem()] * 2 + [vmem()] * 3,
+        out_specs=(vmem(),) * 3 + (smem(),) * 2,
         scratch_shapes=[
             pltpu.VMEM((BLK, BLK), jnp.float32),
-            pltpu.VMEM((BLK, LANES), jnp.float32),
-            pltpu.VMEM((BLK, LANES), jnp.float32),
-            pltpu.VMEM((eblocks, 8, BLK), jnp.float32),
-            pltpu.VMEM((eblocks, 8, BLK), jnp.float32),
+            pltpu.VMEM((BLK, BLK), jnp.float32),
+            pltpu.VMEM((seekers + BLK, LANES), jnp.float32),
+            pltpu.VMEM((seekers + BLK, LANES), jnp.float32),
+            pltpu.VMEM((eblocks + 1, 8, BLK), jnp.float32),
+            pltpu.VMEM((eblocks + 1, 8, BLK), jnp.float32),
         ],
         compiler_params=pltpu.CompilerParams(vmem_limit_bytes=VMEM_LIMIT),
         name="stats",
-    )(flags, seeker_emb, employer_emb, bilinear)
-
-    row_top, row_coef, col_top, col_coef = pl.pallas_call(
+    )(seek_region, emp_region, seeker_emb, employer_emb, bilinear)
+
+    row_pack, col_pack = pl.pallas_call(
         functools.partial(exchange_kernel, n_seek, n_emp),
-        out_shape=(f32(nblocks, BLK), f32(nblocks, BLK), f32(eblocks, BLK), f32(eblocks, BLK)),
-        in_specs=[vmem()] * 4,
-        out_specs=(vmem(),) * 4,
+        out_shape=(f32(nblocks, 8, BLK), f32(eblocks, 8, BLK)),
+        in_specs=[vmem()] * 6,
+        out_specs=(vmem(),) * 2,
         scratch_shapes=[
             pltpu.VMEM((n_emp, 2, nblocks, BLK), jnp.float32),
             pltpu.VMEM((n_seek, 2, eblocks, BLK), jnp.float32),
@@ -414,34 +494,31 @@
         ],
         compiler_params=pltpu.CompilerParams(collective_id=0, has_side_effects=True),
         name="exchange",
-    )(row_stats, col_stats, row_weight, col_weight)
+    )(
+        row_stats, col_stats, seek_weight.reshape(1, seekers), emp_weight.reshape(1, employers),
+        logged_emp.reshape(1, seekers), logged_seeker.reshape(1, employers),
+    )
 
     pulled, back = pl.pallas_call(
         functools.partial(grad_kernel, nblocks, eblocks),
-        out_shape=(f32(seekers, E), f32(employers, E)),
-        in_specs=[smem()] + [vmem()] * 10,
+        out_shape=(f32(seekers + BLK, E), f32(employers + BLK, E)),
+        in_specs=[smem()] * 2 + [vmem()] * 4,
         out_specs=(vmem(),) * 2,
-        scratch_shapes=[
-            pltpu.VMEM((BLK, BLK), jnp.float32),
-            pltpu.VMEM((BLK, BLK), jnp.bfloat16),
-        ]
-        + [pltpu.VMEM((BLK, LANES), jnp.float32)] * 4,
+        scratch_shapes=[pltpu.VMEM((BLK, BLK), jnp.float32)] * 2
+        + [pltpu.VMEM((BLK, BLK), jnp.bfloat16)] * 2
+        + [pltpu.VMEM((seekers, LANES), jnp.float32)] * 4,
         compiler_params=pltpu.CompilerParams(vmem_limit_bytes=VMEM_LIMIT),
         name="grads",
-    )(
-        flags, proj, employer_emb,
-        row_top, row_coef, row_weight, row_log, col_top, col_coef, col_weight, col_log,
-    )
+    )(list_i, list_j, proj, employer_emb, row_pack, col_pack)
 
     share = seekers // n_emp
     eshare = employers // n_seek
-    own_rows = lax.dynamic_slice_in_dim(seeker_emb, emp_pos * share, share, 0)
     slab = E // n_emp
     dma = pltpu.SemaphoreType.DMA
     return pl.pallas_call(
         functools.partial(reduce_kernel, n_seek, n_emp),
         out_shape=(f32(share, E), f32(eshare, E), f32(E, E)),
-        in_specs=[vmem()] * 4,
+        in_specs=[vmem()] * 2 + [pl.BlockSpec(memory_space=pl.ANY), vmem()],
         out_specs=(vmem(),) * 3,
         scratch_shapes=[
             pltpu.VMEM((n_emp // 2, share, E), jnp.float32),
@@ -459,12 +536,13 @@
             dma((n_emp,)), dma((n_emp,)),
             dma((n_seek,)), dma((n_seek,)),
             dma((n_emp,)), dma((n_emp,)),
+            pltpu.VMEM((share, E), jnp.bfloat16), dma,
         ],
         compiler_params=pltpu.CompilerParams(
             collective_id=1, has_side_effects=True, vmem_limit_bytes=VMEM_LIMIT
         ),
         name="reduce",
-    )(pulled, back, own_rows, bilinear)
+    )(pulled, back, seeker_emb, bilinear)
 
 
 def solution(mesh):

time: 185 us -> 179 us (0.968)
  local copies, waits for them, and re-layouts: 11.7 us -> 5.27 us
    pallas_call x1, Pallas kernels: 34.3 us -> 45.5 us  [body(): pl.pallas_call(functools.partial(grad_kernel, nblocks, eblocks), out_shap...]
    pallas_call x1, Pallas kernels: 95.1 us -> 86.6 us  [body(): pl.pallas_call(functools.partial(reduce_kernel, n_seek, n_emp), out_shape...]
    pallas_call x1, Pallas kernels: 14.6 us -> 10.3 us  [body(): pl.pallas_call(functools.partial(exchange_kernel, n_seek, n_emp), out_sha...]
    dynamic_slice x3 -> x0, local copies, waits for them, and re-layouts: 3.34 us -> none  [the longest x1 1.87 us: body(): own_rows = lax.dynamic_slice_in_dim(seeker_emb, emp_pos * share, share, 0)]
    pallas_call x1, Pallas kernels: 27.6 us -> 30.5 us  [body(): pl.pallas_call(functools.partial(stats_kernel, nblocks, eblocks), out_sha...]
    reshape x4 -> x0, local copies, waits for them, and re-layouts: 2.46 us -> none  [the longest x1 0.62 us: body(): row_weight = (seek_weight * scale).reshape(nblocks, BLK)]
    unnamed x13 -> x5, local copies, waits for them, and re-layouts: 5.29 us -> 5.27 us
where the time goes in v2:
time: 179 us
  Pallas kernels  173 us (97%)
  local copies, waits for them, and re-layouts  5.27 us (3%)
    pallas_call x1, Pallas kernels, body(): pl.pallas_call(functools.partial(reduce_kernel, n_seek, n_emp), out_shape...  86.6 us
    pallas_call x1, Pallas kernels, body(): pl.pallas_call(functools.partial(grad_kernel, nblocks, eblocks), out_shap...  45.5 us
    pallas_call x1, Pallas kernels, body(): pl.pallas_call(functools.partial(stats_kernel, nblocks, eblocks), out_sha...  30.5 us
    pallas_call x1, Pallas kernels, body(): pl.pallas_call(functools.partial(exchange_kernel, n_seek, n_emp), out_sha...  10.3 us
    unnamed x5, local copies, waits for them, and re-layouts  5.27 us

profile of v2, /device:TPU:0, one launch (start us, length us, event | category | flops | bytes accessed | tf_op | source)
XLA Modules:
  0.0 178.8 jit_solution(11955198410649114084)
XLA Ops:
  0.6 30.5 %stats.1 = (bf16[8192,256]{1,0:T(8,128)(2,1)}, f32[2,16,512]{2,1,0:T(8,128)}, f32[2,8,512]{2,1,0:T(8,128)}, s32[133]{0:T(256)}, s32[133]{0:T(256)}) custom-call(s32[64]{0:T(128)} %seek_region.1, s32[64]{0:T(128)} %emp_region.1, bf16[8192,256]{1,0:T(8,128)(2,1)} %seeker.3, bf16[4096,256]{1,0:T(8,128)(2,1)} %employer.3, bf16[256,256]{1,0:T(8,128)(2,1)} %bilinear.3), custom_call_target="tpu_custom_call" | custom-call | tf_op jit(solution)/shard_map/stats/pallas_call | solution.py:459
  31.1 10.3 %exchange.1 = (f32[16,8,512]{2,1,0:T(8,128)}, f32[8,8,512]{2,1,0:T(8,128)}) custom-call(f32[2,16,512]{2,1,0:T(8,128)} %get-tuple-element.15.row_stats, f32[2,8,512]{2,1,0:T(8,128)} %get-tuple-element.16.col_stats, f32[1,8192]{1,0:T(1,128)} %bitcast.4, f32[1,4096]{1,0:T(1,128)} %bitcast.6, s32[1,8192]{1,0:T(1,128)} %bitcast.5, s32[1,4096]{1,0:T(1,128)} %bitcast.7), custom_call_target="tpu_custom_call" | custom-call | tf_op jit(solution)/shard_map/exchange/pallas_call | solution.py:482
  41.4 45.5 %grads.1 = (f32[8704,256]{1,0:T(8,128)}, f32[4608,256]{1,0:T(8,128)}) custom-call(s32[133]{0:T(256)} %get-tuple-element.12.list_i, s32[133]{0:T(256)} %get-tuple-element.13.list_j, bf16[8192,256]{1,0:T(8,128)(2,1)} %get-tuple-element.14.proj, bf16[4096,256]{1,0:T(8,128)(2,1)} %employer.3, f32[16,8,512]{2,1,0:T(8,128)} %get-tuple-element.17.row_pack, ...), custom_call_target="tpu_custom_call" | custom-call | tf_op jit(solution)/shard_map/grads/pallas_call | solution.py:502
  87.0 86.6 %reduce.1 = (f32[1024,256]{1,0:T(8,128)}, f32[1024,256]{1,0:T(8,128)}, f32[256,256]{1,0:T(8,128)}) custom-call(f32[8704,256]{1,0:T(8,128)} %get-tuple-element.19.pulled, f32[4608,256]{1,0:T(8,128)} %get-tuple-element.20.back, bf16[8192,256]{1,0:T(8,128)(2,1)} %seeker.3, bf16[256,256]{1,0:T(8,128)(2,1)} %bilinear.3), custom_call_target="tpu_custom_call" | custom-call | tf_op jit(solution)/shard_map/reduce/pallas_call | solution.py:518
  173.6 0.0 copy-start
  173.6 2.3 %copy.15 = f32[1024,256]{1,0:T(8,128)} copy(f32[1024,256]{1,0:T(8,128)} %get-tuple-element.24) | data formatting | bytes 2097152
  175.9 2.3 %copy.16 = f32[1024,256]{1,0:T(8,128)} copy(f32[1024,256]{1,0:T(8,128)} %get-tuple-element.25) | data formatting | bytes 2097152
  178.1 0.0 copy-done
  178.1 0.7 copy.17
Async XLA Ops:
  173.6 4.6 %copy-start = (f32[256,256]{1,0:T(8,128)S(1)}, f32[256,256]{1,0:T(8,128)}, u32[]{:S(2)}) copy-start(f32[256,256]{1,0:T(8,128)} %get-tuple-element.26) | copy-start | bytes 786436

commit v3 on v2

--- a/solution.py
+++ b/solution.py
@@ -33,15 +33,17 @@
     list_i[0] = nblocks
     list_j[0] = eblocks
 
-    def visit(p, count):
-        i = p // eblocks
-        j = lax.rem(p, eblocks)
-        list_i[count + 1] = i
-        list_j[count + 1] = j
-        same = seek_region[seek_at + i] == emp_region[emp_at + j]
-        return count + same.astype(jnp.int32)
-
-    count = lax.fori_loop(0, nblocks * eblocks, visit, jnp.int32(0))
+    wanted = [emp_region[emp_at + j] for j in range(eblocks)]
+
+    def visit(i, count):
+        region = seek_region[seek_at + i]
+        for j in range(eblocks):
+            list_i[count + 1] = i
+            list_j[count + 1] = j
+            count = count + (region == wanted[j]).astype(jnp.int32)
+        return count
+
+    count = lax.fori_loop(0, nblocks, visit, jnp.int32(0))
     for k in range(1, 4):
         list_i[count + k] = nblocks
         list_j[count + k] = eblocks
@@ -290,21 +292,33 @@
 
 
 def reduce_kernel(
-    n_seek, n_emp, pulled, back, seeker, bilinear,
-    seeker_grad, employer_grad, bilinear_grad,
+    n_seek, n_emp, pulled, back, seeker,
+    share_out, employer_grad, bilinear_grad,
     pair_buf, emp_buf, right_buf, left_buf, bil, bil_emp, bil_seek, bil_all,
     pair_send, pair_recv, emp_send, emp_recv, right_send, right_recv, left_send, left_recv,
     b1_send, b1_recv, b2_send, b2_recv, b3_send, b3_recv, own_rows, own_sem,
+    own_pull, own_pull_sem, own_back, own_back_sem,
 ):
     me_s = lax.axis_index("seek")
     me_e = lax.axis_index("emp")
-    share = seeker_grad.shape[0]
+    share = share_out.shape[0]
     eshare = employer_grad.shape[0]
     half = n_emp // 2
     mine = me_e // 2
     parity = lax.rem(me_e, 2)
     partner = me_e + 1 - 2 * parity
     mirror = n_seek - 1 - me_s
+    fetch_rows = pltpu.make_async_copy(seeker.at[block_ds(me_e, share), :], own_rows, own_sem)
+    fetch_back = pltpu.make_async_copy(
+        back.at[pl.ds(0, eshare * n_seek), :], own_back, own_back_sem
+    )
+    fetch_pull = [
+        pltpu.make_async_copy(
+            pulled.at[block_ds(2 * lax.rem(mine + k, half) + parity, share), :],
+            own_pull.at[k], own_pull_sem.at[k],
+        )
+        for k in range(half)
+    ]
     entry_barrier(n_seek, n_emp, me_s, me_e)
 
     def right_copy(k, src):
@@ -332,12 +346,10 @@
                 @pl.when(jnp.logical_and(pos > 0, pos <= k))
                 def _(make=make, buf=buf, target=target):
                     make(k - 1, buf.at[k - 1]).wait_recv()
-                    buf[k - 1] += back[block_ds(target, eshare), :]
+                    buf[k - 1] += own_back[block_ds(target, eshare), :]
                     make(k, buf.at[k - 1]).start()
 
     line_step(0)
-    fetch = pltpu.make_async_copy(seeker.at[block_ds(me_e, share), :], own_rows, own_sem)
-    fetch.start()
     pairs = []
     order = list(range(half - 1, -1, -1))
     for k in range(half):
@@ -348,16 +360,22 @@
         ))
     for k in order:
         pairs[k].start()
+    for k in order:
+        fetch_pull[k].start()
+    fetch_back.start()
+    fetch_rows.start()
     seconds = {}
     for k in order:
         pairs[k].wait_recv()
         target = 2 * lax.rem(mine + k, half) + parity
-        pair_buf[k] += pulled[block_ds(target, share), :]
+        fetch_pull[k].wait()
+        pair_buf[k] += own_pull[k]
         if k > 0:
             seconds[k] = send(
                 pair_buf.at[k], emp_buf.at[k], emp_send.at[k], emp_recv.at[k], "emp", target
             )
             seconds[k].start()
+    fetch_back.wait()
     for k in range(1, n_seek - 1):
         line_step(k)
     for k in seconds:
@@ -365,7 +383,8 @@
         pair_buf[0] += emp_buf[k]
 
     share_rows = pair_buf[0].astype(jnp.bfloat16)
-    fetch.wait()
+    share_out[...] = share_rows
+    fetch_rows.wait()
     bil[...] = tn_dot(own_rows[...], share_rows)
     slab = E // n_emp
     b1 = []
@@ -377,7 +396,6 @@
         ))
     for copy in b1:
         copy.start()
-    seeker_grad[...] = nt_dot(share_rows, bilinear[...])
     own_slab = block_ds(me_e, slab)
     for copy in b1:
         copy.wait_recv()
@@ -417,7 +435,7 @@
         ).wait_recv()
     bilinear_grad[...] = bil_all[...]
 
-    employer_grad[...] = back[block_ds(me_s, eshare), :]
+    employer_grad[...] = own_back[block_ds(me_s, eshare), :]
     last = n_seek - 2
     for pos, make, buf in ((me_s, right_copy, right_buf), (mirror, left_copy, left_buf)):
         @pl.when(pos > 0)
@@ -432,6 +450,14 @@
             @pl.when(pos <= k)
             def _(k=k, make=make, buf=buf):
                 make(k, buf.at[k]).wait_send()
+
+
+def finish_kernel(
+    share_rows, bilinear, employer_part, bilinear_part, seeker_grad, employer_grad, bilinear_grad
+):
+    seeker_grad[...] = nt_dot(share_rows[...], bilinear[...])
+    employer_grad[...] = employer_part[...]
+    bilinear_grad[...] = bilinear_part[...]
 
 
 def vmem():
@@ -515,10 +541,12 @@
     eshare = employers // n_seek
     slab = E // n_emp
     dma = pltpu.SemaphoreType.DMA
-    return pl.pallas_call(
+    share_rows, employer_part, bilinear_part = pl.pallas_call(
         functools.partial(reduce_kernel, n_seek, n_emp),
-        out_shape=(f32(share, E), f32(eshare, E), f32(E, E)),
-        in_specs=[vmem()] * 2 + [pl.BlockSpec(memory_space=pl.ANY), vmem()],
+        out_shape=(
+            jax.ShapeDtypeStruct((share, E), jnp.bfloat16), f32(eshare, E), f32(E, E)
+        ),
+        in_specs=[pl.BlockSpec(memory_space=pl.ANY)] * 3,
         out_specs=(vmem(),) * 3,
         scratch_shapes=[
             pltpu.VMEM((n_emp // 2, share, E), jnp.float32),
@@ -537,12 +565,21 @@
             dma((n_seek,)), dma((n_seek,)),
             dma((n_emp,)), dma((n_emp,)),
             pltpu.VMEM((share, E), jnp.bfloat16), dma,
+            pltpu.VMEM((n_emp // 2, share, E), jnp.float32), dma((n_emp // 2,)),
+            pltpu.VMEM((employers, E), jnp.float32), dma,
         ],
         compiler_params=pltpu.CompilerParams(
             collective_id=1, has_side_effects=True, vmem_limit_bytes=VMEM_LIMIT
         ),
         name="reduce",
-    )(pulled, back, seeker_emb, bilinear)
+    )(pulled, back, seeker_emb)
+    return pl.pallas_call(
+        finish_kernel,
+        out_shape=(f32(share, E), f32(eshare, E), f32(E, E)),
+        in_specs=[vmem()] * 4,
+        out_specs=(vmem(),) * 3,
+        name="finish",
+    )(share_rows, bilinear, employer_part, bilinear_part)
 
 
 def solution(mesh):

time: 179 us -> 176 us (0.983)
  local copies, waits for them, and re-layouts: 5.27 us -> 0 us
    unnamed x5 -> x0, local copies, waits for them, and re-layouts: 5.27 us -> none
    pallas_call x1, Pallas kernels: 86.6 us -> 82.2 us  [body(): pl.pallas_call(functools.partial(reduce_kernel, n_seek, n_emp), out_shape...]
    pallas_call x0 -> x1, Pallas kernels: none -> 3.23 us  [body(): pl.pallas_call(finish_kernel, out_shape=(f32(share, E), f32(eshare, E), f...]
    pallas_call x1, Pallas kernels: 10.3 us -> 13.1 us  [body(): pl.pallas_call(functools.partial(exchange_kernel, n_seek, n_emp), out_sha...]
where the time goes in v3:
time: 176 us; the launch traced here: 174 us
  Pallas kernels  173 us (98%)
    pallas_call x1, Pallas kernels, body(): pl.pallas_call(functools.partial(reduce_kernel, n_seek, n_emp), out_shape...  82.2 us
    pallas_call x1, Pallas kernels, body(): pl.pallas_call(functools.partial(grad_kernel, nblocks, eblocks), out_shap...  45.6 us
    pallas_call x1, Pallas kernels, body(): pl.pallas_call(functools.partial(stats_kernel, nblocks, eblocks), out_sha...  29.2 us
    pallas_call x1, Pallas kernels, body(): pl.pallas_call(functools.partial(exchange_kernel, n_seek, n_emp), out_sha...  13.1 us

profile of v3, /device:TPU:0, one launch (start us, length us, event | category | flops | bytes accessed | tf_op | source)
XLA Modules:
  0.0 174.1 jit_solution(6165466144585856431)
XLA Ops:
  0.6 29.2 %stats.1 = (bf16[8192,256]{1,0:T(8,128)(2,1)}, f32[2,16,512]{2,1,0:T(8,128)}, f32[2,8,512]{2,1,0:T(8,128)}, s32[133]{0:T(256)}, s32[133]{0:T(256)}) custom-call(s32[64]{0:T(128)} %seek_region.1, s32[64]{0:T(128)} %emp_region.1, bf16[8192,256]{1,0:T(8,128)(2,1)} %seeker.3, bf16[4096,256]{1,0:T(8,128)(2,1)} %employer.3, bf16[256,256]{1,0:T(8,128)(2,1)} %bilinear.3), custom_call_target="tpu_custom_call" | custom-call | tf_op jit(solution)/shard_map/stats/pallas_call | solution.py:485
  29.9 13.1 %exchange.1 = (f32[16,8,512]{2,1,0:T(8,128)}, f32[8,8,512]{2,1,0:T(8,128)}) custom-call(f32[2,16,512]{2,1,0:T(8,128)} %get-tuple-element.18.row_stats, f32[2,8,512]{2,1,0:T(8,128)} %get-tuple-element.19.col_stats, f32[1,8192]{1,0:T(1,128)} %bitcast.4, f32[1,4096]{1,0:T(1,128)} %bitcast.6, s32[1,8192]{1,0:T(1,128)} %bitcast.5, s32[1,4096]{1,0:T(1,128)} %bitcast.7), custom_call_target="tpu_custom_call" | custom-call | tf_op jit(solution)/shard_map/exchange/pallas_call | solution.py:508
  43.0 45.6 %grads.1 = (f32[8704,256]{1,0:T(8,128)}, f32[4608,256]{1,0:T(8,128)}) custom-call(s32[133]{0:T(256)} %get-tuple-element.15.list_i, s32[133]{0:T(256)} %get-tuple-element.16.list_j, bf16[8192,256]{1,0:T(8,128)(2,1)} %get-tuple-element.17.proj, bf16[4096,256]{1,0:T(8,128)(2,1)} %employer.3, f32[16,8,512]{2,1,0:T(8,128)} %get-tuple-element.20.row_pack, ...), custom_call_target="tpu_custom_call" | custom-call | tf_op jit(solution)/shard_map/grads/pallas_call | solution.py:528
  88.6 82.2 %reduce.1 = (bf16[1024,256]{1,0:T(8,128)(2,1)}, f32[1024,256]{1,0:T(8,128)}, f32[256,256]{1,0:T(8,128)}) custom-call(f32[8704,256]{1,0:T(8,128)} %get-tuple-element.22.pulled, f32[4608,256]{1,0:T(8,128)} %get-tuple-element.23.back, bf16[8192,256]{1,0:T(8,128)(2,1)} %seeker.3), custom_call_target="tpu_custom_call" | custom-call | tf_op jit(solution)/shard_map/reduce/pallas_call | solution.py:544
  170.8 3.2 %finish.1 = (f32[1024,256]{1,0:T(8,128)}, f32[1024,256]{1,0:T(8,128)}, f32[256,256]{1,0:T(8,128)}) custom-call(bf16[1024,256]{1,0:T(8,128)(2,1)} %get-tuple-element.24.share_rows, bf16[256,256]{1,0:T(8,128)(2,1)} %bilinear.3, f32[1024,256]{1,0:T(8,128)} %get-tuple-element.25.employer_part, f32[256,256]{1,0:T(8,128)} %get-tuple-element.26.bilinear_part), custom_call_target="tpu_custom_call" | custom-call | tf_op jit(solution)/shard_map/finish/pallas_call | solution.py:576
